TPU v7x, 512 devices: a whole 4x8x8 slice. The times are simulated.
512 devices in a mesh: blk: 8 (over y_lo, core), team: 64 (over y_hi, x, z).
Axes of the slice: x: 4, y: 8 (y_hi: 2, y_lo: 4; y = y_hi * 4 + y_lo), z: 8, core: 2. Of those that a mesh axis runs over, the one named last changes fastest.
Arguments:
- features: bfloat16 [65536, 256], P(('blk', 'team')), may hold values from -6 to 6
- weight: bfloat16 [256, 256], replicated, may hold values from -0.375 to 0.375
- bias: float32 [256], replicated, may hold values from -3 to 3
- cotangent: bfloat16 [65536, 256], P(('blk', 'team')), may hold values from -6 to 6
- adj_cols: int32 [64, 8, 8, 12], P('team', None, 'blk'), may hold values from 0 to 63, as said below
- adj_vals: bfloat16 [64, 8, 8, 12, 128, 128], P('team', None, 'blk'), as said below
Outputs:
- hidden: bfloat16 [65536, 256], P(('blk', 'team'))
- grad_input: bfloat16 [65536, 256], P(('blk', 'team'))
- grad_weight: float32 [256, 256], replicated
- grad_bias: float32 [256], replicated
Inputs may be any that keep to these rules, and one draw needn't show every extreme that they name: `adj_cols`: for every node panel and column group the 12 entries are distinct. Block (i, j) of A is listed exactly when block (j, i) is, every column panel is listed by exactly 12 row panels of each column group, and A is symmetric. `adj_vals`: the block listed for panels (i, j) is the transpose of the block listed for (j, i), so A is symmetric.
All inputs are finite; a program needn't handle non-finite values.
Results may differ from a plain program's by a relative error of at most 0.0075.
Values may be sent and summed in bfloat16 or wider, within the bound.
No kernel may reach another device: no remote copies, remote signals or barrier semaphores. Data moves between devices by JAX's collectives and lax.ppermute only.
A program may use at most 64 MiB of HBM per device.

v0:
```python
import jax
import jax.numpy as jnp
from jax import lax
from jax.sharding import Mesh
from jax.sharding import PartitionSpec as P

BLK_AXES = ("y_lo", "core")
TEAM_AXES = ("y_hi", "x", "z")
PLANE = ("x", "z")
ALL_AXES = BLK_AXES + TEAM_AXES


def fine_mesh(mesh):
    blk = mesh.shape["blk"]
    team = mesh.shape["team"]
    sizes = (blk // 2, 2, 2, 4, team // 8)
    return Mesh(mesh.devices.reshape(sizes), ALL_AXES)


def gather_team(rows):
    other = lax.ppermute(rows, "y_hi", perm=[(0, 1), (1, 0)])
    pair = jnp.stack([rows, other], axis=0)
    full = lax.all_gather(pair, PLANE, axis=0, tiled=True)
    return full.reshape(-1, rows.shape[1])


def member_slots(members, plane_size):
    my_hi = lax.axis_index("y_hi")
    return members % plane_size * 2 + (members // plane_size != my_hi).astype(jnp.int32)


def collect(panels, slots, adj_vals):
    block = adj_vals.shape[-1]
    width = panels.shape[1]
    stacked = panels.reshape(panels.shape[0] // block, block, width)
    picked = jnp.take(stacked, slots, axis=0)
    summed = jnp.einsum(
        "rkij,rkjf->rif", adj_vals[0, :, 0], picked, preferred_element_type=jnp.float32
    )
    return summed.reshape(-1, width)


def activation(value):
    return jax.nn.gelu(value, approximate=True)


def local(features, weight, bias, cotangent, adj_cols, adj_vals):
    plane_size = lax.psum(1, PLANE)
    slots = member_slots(adj_cols[0, :, 0, :], plane_size)
    product = jnp.dot(features, weight, preferred_element_type=jnp.float32).astype(jnp.bfloat16)
    gathered = gather_team(product)
    partial_rows = collect(gathered, slots, adj_vals)
    summed = lax.psum_scatter(partial_rows, BLK_AXES, scatter_dimension=0, tiled=True)
    pre = summed + bias[None, :]
    activated, pullback = jax.vjp(activation, pre)
    hidden = activated.astype(jnp.bfloat16)
    pulled = pullback(cotangent.astype(jnp.float32))[0].astype(jnp.bfloat16)
    pulled_group = gather_team(pulled)
    partial_back = collect(pulled_group, slots, adj_vals)
    spread = lax.psum_scatter(partial_back, BLK_AXES, scatter_dimension=0, tiled=True).astype(
        jnp.bfloat16
    )
    grad_input = jnp.dot(spread, weight.T, preferred_element_type=jnp.float32).astype(jnp.bfloat16)
    local_weight = lax.dot_general(
        features, spread, (((0,), (0,)), ((), ())), preferred_element_type=jnp.float32
    )
    local_bias = jnp.sum(pulled.astype(jnp.float32), axis=0)
    both = jnp.concatenate([local_weight, local_bias[None, :]], axis=0)
    both = lax.psum(both, PLANE)
    both = lax.psum(both, ("y_lo", "y_hi", "core"))
    grad_weight = both[:-1]
    grad_bias = both[-1]
    return (hidden, grad_input, grad_weight, grad_bias)


def solution(mesh):
    fine = fine_mesh(mesh)
    rows = P(ALL_AXES, None)
    return jax.shard_map(
        local,
        mesh=fine,
        in_specs=(
            rows,
            P(),
            P(),
            rows,
            P(TEAM_AXES, None, BLK_AXES, None),
            P(TEAM_AXES, None, BLK_AXES, None, None, None),
        ),
        out_specs=(rows, rows, P(), P()),
        check_vma=False,
    )
```

profile of v0, /device:TPU:1, one launch (start us, length us, event | category | flops | bytes accessed | tf_op | source)
XLA Modules:
  0.0 590.6 jit_solution(9726838023997011577)
XLA Ops:
  7.2 0.0 all-gather.3.cloned.1.call-start
  7.2 1.2 convolution_convert_fusion.1
  8.5 8.3 %collective-permute-start = (bf16[128,256]{1,0:T(8,128)(2,1)S(1)}, bf16[128,256]{1,0:T(8,128)(2,1)S(1)}, u32[]{:S(2)}, u32[]{:S(2)}) collective-permute-start(bf16[128,256]{1,0:T(8,128)(2,1)S(1)} %convolution_convert_fusion.1), channel_id=1, source_target_pairs={{0,32},{32,0},{1,33},{33,1},{2,34},{34,2},{3,35},{35,3},{4,36},{36... | collective-permute-start | bytes 196616 | tf_op jit(solution)/shard_map/ppermute | solution.py:21
  16.8 1.7 collective-permute-done
  18.5 0.7 pad_maximum_fusion.1
  19.1 0.0 all-gather.3.cloned.1.call-update
  19.2 0.0 reduce-scatter.3.cloned.1.call-start
  19.2 0.7 compare_and_fusion
  19.9 0.1 reshape.42
  20.0 91.1 %all-gather.3.cloned.1.call-done = bf16[64,128,256]{2,1,0:T(8,128)(2,1)} async-done(((bf16[2,128,256]{2,1,0:T(8,128)(2,1)}), bf16[64,128,256]{2,1,0:T(8,128)(2,1)}) %all-gather.3.cloned.1.call-update) | async-done | bytes 4194320 | tf_op jit(solution)/shard_map/all_gather | solution.py:23
  111.1 8.2 %gather_fusion = bf16[96,128,256]{2,1,0:T(8,128)(2,1)} fusion(bf16[64,128,256]{2,1,0:T(8,128)(2,1)} %all-gather.3.cloned.1.call-done, s32[1024]{0:T(1024)S(1)} %pad_clamp_fusion), kind=kCustom, calls=%fused_computation.clone | custom fusion | bytes 12583296 | tf_op jit(solution)/shard_map/jit(_take)/gather | solution.py:36
  119.3 5.2 fusion.2
  124.5 0.0 all-gather.5.cloned.1.call-start
  124.6 38.0 %reduce-scatter.3.cloned.1.call-done = f32[128,256]{1,0:T(8,128)} async-done(((f32[1024,256]{1,0:T(8,128)}), f32[128,256]{1,0:T(8,128)}) %reduce-scatter.3.cloned.1.call-update) | async-done | bytes 131088 | tf_op jit(solution)/shard_map/reduce_scatter | solution.py:53
  162.5 1.6 convert_reduce_fusion
  164.2 5.5 collective-permute-start.1
  169.6 3.7 collective-permute-done.1
  173.3 0.7 pad_maximum_fusion.2
  174.0 0.0 reduce-scatter.5.cloned.1.call-start
  174.1 86.9 %all-gather.5.cloned.1.call-done = bf16[64,128,256]{2,1,0:T(8,128)(2,1)} async-done(((bf16[2,128,256]{2,1,0:T(8,128)(2,1)}), bf16[64,128,256]{2,1,0:T(8,128)(2,1)}) %all-gather.5.cloned.1.call-update) | async-done | bytes 4194320 | tf_op jit(solution)/shard_map/all_gather | solution.py:23
  260.9 8.2 %gather_fusion.1 = bf16[96,128,256]{2,1,0:T(8,128)(2,1)} fusion(bf16[64,128,256]{2,1,0:T(8,128)(2,1)} %all-gather.5.cloned.1.call-done, s32[1024]{0:T(1024)S(1)} %pad_clamp_fusion), kind=kCustom, calls=%fused_computation.1.clone | custom fusion | bytes 12583296 | tf_op jit(solution)/shard_map/jit(_take)/gather | solution.py:36
  269.1 5.2 fusion
  274.3 0.0 all-reduce.3.cloned.1.call-start
  274.4 38.0 %reduce-scatter.5.cloned.1.call-done = f32[128,256]{1,0:T(8,128)} async-done(((f32[1024,256]{1,0:T(8,128)}), f32[128,256]{1,0:T(8,128)}) %reduce-scatter.5.cloned.1.call-update) | async-done | bytes 131088 | tf_op jit(solution)/shard_map/reduce_scatter | solution.py:60
  312.3 1.1 convolution_bitcast_fusion
  313.5 0.7 pad_maximum_fusion
  314.2 0.0 all-reduce.5.cloned.1.call-start
  314.3 153.2 %all-reduce.3.cloned.1.call-done = f32[257,256]{1,0:T(8,128)} async-done(((f32[257,256]{1,0:T(8,128)}), f32[257,256]{1,0:T(8,128)}) %all-reduce.3.cloned.1.call-update) | async-done | bytes 263184 | tf_op jit(solution)/shard_map/psum | solution.py:69
  467.5 1.7 convolution_convert_fusion
  469.2 111.6 %all-reduce.5.cloned.1.call-done = f32[257,256]{1,0:T(8,128)} async-done(((f32[257,256]{1,0:T(8,128)}), f32[257,256]{1,0:T(8,128)}) %all-reduce.5.cloned.1.call-update) | async-done | bytes 263184 | tf_op jit(solution)/shard_map/psum | solution.py:70
  580.8 1.3 slice.13
  582.1 1.7 slice.12
  (16 shorter events, 0.1 us)
Async XLA Ops:
  7.2 112.1 %copy-start = (bf16[1,8,1,12,128,128]{5,4,3,2,1,0:T(8,128)(2,1)S(1)}, bf16[1,8,1,12,128,128]{5,4,3,2,1,0:T(8,128)(2,1)}, u32[]{:S(2)}) copy-start(bf16[1,8,1,12,128,128]{5,4,3,2,1,0:T(8,128)(2,1)} %param.13) | copy-start | bytes 9437188
  7.2 103.9 %all-gather.3.cloned.1.call-start = ((), (), s32[]{:S(2)}) async-start(), calls=%async_computation.2 | async-start | bytes 4325376 | tf_op jit(solution)/shard_map/all_gather | solution.py:23
  8.5 10.0 %collective-permute-start = (bf16[128,256]{1,0:T(8,128)(2,1)S(1)}, bf16[128,256]{1,0:T(8,128)(2,1)S(1)}, u32[]{:S(2)}, u32[]{:S(2)}) collective-permute-start(bf16[128,256]{1,0:T(8,128)(2,1)S(1)} %convolution_convert_fusion.1), channel_id=1, source_target_pairs={{0,32},{32,0},{1,33},{33,1},{2,34},{34,2},{3,35},{35,3},{4,36},{36... | collective-permute-start | bytes 196616 | tf_op jit(solution)/shard_map/ppermute | solution.py:21
  19.2 143.4 %reduce-scatter.3.cloned.1.call-start = ((), (), s32[]{:S(2)}) async-start(), calls=%async_computation.3 | async-start | bytes 1179648 | tf_op jit(solution)/shard_map/reduce_scatter | solution.py:53
  119.3 43.2 %copy-start.3 = (bf16[128,256]{1,0:T(8,128)(2,1)S(1)}, bf16[128,256]{1,0:T(8,128)(2,1)}, u32[]{:S(2)}) copy-start(bf16[128,256]{1,0:T(8,128)(2,1)} %param.11) | copy-start | bytes 196612
  119.3 43.2 %copy-start.4 = (f32[256]{0:T(256)S(1)}, f32[256]{0:T(256)}, u32[]{:S(2)}) copy-start(f32[256]{0:T(256)} %param.10) | copy-start | bytes 3076
  124.5 136.4 %all-gather.5.cloned.1.call-start = ((), (), s32[]{:S(2)}) async-start(), calls=%async_computation.4 | async-start | bytes 4325376 | tf_op jit(solution)/shard_map/all_gather | solution.py:23
  164.2 9.1 %collective-permute-start.1 = (bf16[128,256]{1,0:T(8,128)(2,1)S(1)}, bf16[128,256]{1,0:T(8,128)(2,1)S(1)}, u32[]{:S(2)}, u32[]{:S(2)}) collective-permute-start(bf16[128,256]{1,0:T(8,128)(2,1)S(1)} %get-tuple-element.6), channel_id=1, source_target_pairs={{0,32},{32,0},{1,33},{33,1},{2,34},{34,2},{3,35},{35,3},{4,36},{36... | collective-permute-start | bytes 196616 | tf_op jit(solution)/shard_map/ppermute | solution.py:21
  174.0 138.3 %reduce-scatter.5.cloned.1.call-start = ((), (), s32[]{:S(2)}) async-start(), calls=%async_computation.5 | async-start | bytes 1179648 | tf_op jit(solution)/shard_map/reduce_scatter | solution.py:60
  269.1 43.2 %copy-start.2 = (bf16[128,256]{1,0:T(8,128)(2,1)S(1)}, bf16[128,256]{1,0:T(8,128)(2,1)}, u32[]{:S(2)}) copy-start(bf16[128,256]{1,0:T(8,128)(2,1)} %param.8) | copy-start | bytes 196612
  269.1 198.3 %copy-start.1 = (bf16[256,256]{1,0:T(8,128)(2,1)S(1)}, bf16[256,256]{1,0:T(8,128)(2,1)}, u32[]{:S(2)}) copy-start(bf16[256,256]{1,0:T(8,128)(2,1)} %param.9) | copy-start | bytes 393220
  274.3 193.1 %all-reduce.3.cloned.1.call-start = ((), (), s32[]{:S(2)}) async-start(), calls=%async_computation.6 | async-start | bytes 540672 | tf_op jit(solution)/shard_map/psum | solution.py:69
  314.2 266.6 %all-reduce.5.cloned.1.call-start = ((), (), s32[]{:S(2)}) async-start(), calls=%async_computation.7 | async-start | bytes 540672 | tf_op jit(solution)/shard_map/psum | solution.py:70
Sparse Core Ops, SparseCore 0:
  19.3 91.7 all-gather.2
  124.6 37.8 reduce-scatter.2
  174.1 86.7 all-gather.4
  274.5 37.8 reduce-scatter.4
  315.6 151.7 all-reduce.2
  469.6 111.1 all-reduce.4
where the time goes:
time: 591 us
  waiting for transfers between devices  524 us (89%)
  local copies, waits for them, and re-layouts  19.4 us (3%)
  matrix products  14.5 us (2%)
  between operations  14.2 us (2%)
  starting transfers between devices  14 us (2%)
    all_gather x2, waiting for transfers between devices, gather_team(): full = lax.all_gather(pair, PLANE, axis=0, tiled=True)  178 us
    psum x1, waiting for transfers between devices, local(): both = lax.psum(both, PLANE)  153 us
    psum x1, waiting for transfers between devices, local(): both = lax.psum(both, ('y_lo', 'y_hi', 'core'))  112 us
    reduce_scatter x1, waiting for transfers between devices, local(): lax.psum_scatter(partial_back, BLK_AXES, scatter_dimension=0, tiled=True)  38 us
    reduce_scatter x1, waiting for transfers between devices, local(): lax.psum_scatter(partial_rows, BLK_AXES, scatter_dimension=0, tiled=True)  38 us
    gather x2, local copies, waits for them, and re-layouts, collect(): picked = jnp.take(stacked, slots, axis=0)  16.4 us
    ppermute x2, starting transfers between devices, gather_team(): other = lax.ppermute(rows, 'y_hi', perm=[(0, 1), (1, 0)])  13.7 us
  transfers between devices with their start and end apart: 8, of which 8 were waited for; matrix products, arithmetic and copies ran while one was open for 0% of the time, Pallas kernels for 0%

commit v1 on v0

--- a/solution.py
+++ b/solution.py
@@ -20,7 +20,9 @@
 def gather_team(rows):
     other = lax.ppermute(rows, "y_hi", perm=[(0, 1), (1, 0)])
     pair = jnp.stack([rows, other], axis=0)
-    full = lax.all_gather(pair, PLANE, axis=0, tiled=True)
+    full = jnp.concatenate(
+        lax.all_to_all(jnp.stack([pair] * lax.axis_size(PLANE)), PLANE, 0, 0), axis=0
+    )
     return full.reshape(-1, rows.shape[1])
 
 

time: 591 us -> 622 us (1.052)
  blocking collectives: 0 us -> 95 us
  waiting for transfers between devices: 524 us -> 446 us
  starting transfers between devices: 14 us -> 26.9 us
    all_gather x2 -> x0, waiting for transfers between devices: 178 us -> none  [gather_team(): full = lax.all_gather(pair, PLANE, axis=0, tiled=True)]
    all_to_all x0 -> x1, blocking collectives: none -> 95 us  [gather_team(): lax.all_to_all(jnp.stack([pair] * lax.axis_size(PLANE)), PLANE, 0, 0)]
    all_to_all x0 -> x1, waiting for transfers between devices: none -> 94.7 us  [gather_team(): lax.all_to_all(jnp.stack([pair] * lax.axis_size(PLANE)), PLANE, 0, 0)]
    all_to_all x0 -> x1, starting transfers between devices: none -> 13 us  [gather_team(): lax.all_to_all(jnp.stack([pair] * lax.axis_size(PLANE)), PLANE, 0, 0)]
  transfers between devices with their start and end apart: 8 -> 7, of which waited for: 8 -> 7; matrix products, arithmetic and copies ran while one was open for 0% -> 0% of each run, Pallas kernels for 0% -> 0%
where the time goes in v1:
time: 622 us; the launch traced here: 621 us
  waiting for transfers between devices  446 us (72%)
  blocking collectives  95 us (15%)
  starting transfers between devices  26.9 us (4%)
  local copies, waits for them, and re-layouts  22.4 us (4%)
  matrix products  14.5 us (2%)
  between operations  13.9 us (2%)
    psum x1, waiting for transfers between devices, local(): both = lax.psum(both, PLANE)  153 us
    psum x1, waiting for transfers between devices, local(): both = lax.psum(both, ('y_lo', 'y_hi', 'core'))  112 us
    all_to_all x1, blocking collectives, gather_team(): lax.all_to_all(jnp.stack([pair] * lax.axis_size(PLANE)), PLANE, 0, 0)  95 us
    all_to_all x1, waiting for transfers between devices, gather_team(): lax.all_to_all(jnp.stack([pair] * lax.axis_size(PLANE)), PLANE, 0, 0)  94.7 us
    reduce_scatter x1, waiting for transfers between devices, local(): lax.psum_scatter(partial_back, BLK_AXES, scatter_dimension=0, tiled=True)  44 us
    reduce_scatter x1, waiting for transfers between devices, local(): lax.psum_scatter(partial_rows, BLK_AXES, scatter_dimension=0, tiled=True)  37 us
    gather x2, local copies, waits for them, and re-layouts, collect(): picked = jnp.take(stacked, slots, axis=0)  16.4 us
    ppermute x2, starting transfers between devices, gather_team(): other = lax.ppermute(rows, 'y_hi', perm=[(0, 1), (1, 0)])  13.8 us
  transfers between devices with their start and end apart: 7, of which 7 were waited for; matrix products, arithmetic and copies ran while one was open for 0% of the time, Pallas kernels for 0%

profile of v1, /device:TPU:1, one launch (start us, length us, event | category | flops | bytes accessed | tf_op | source)
XLA Modules:
  0.0 621.3 jit_solution(13930558632110600693)
XLA Ops:
  7.2 1.2 convolution_convert_fusion.1
  8.4 8.3 %collective-permute-start = (bf16[128,256]{1,0:T(8,128)(2,1)S(1)}, bf16[128,256]{1,0:T(8,128)(2,1)S(1)}, u32[]{:S(2)}, u32[]{:S(2)}) collective-permute-start(bf16[128,256]{1,0:T(8,128)(2,1)S(1)} %convolution_convert_fusion.1), channel_id=1, source_target_pairs={{0,32},{32,0},{1,33},{33,1},{2,34},{34,2},{3,35},{35,3},{4,36},{36... | collective-permute-start | bytes 196616 | tf_op jit(solution)/shard_map/ppermute | solution.py:21
  16.7 1.7 collective-permute-done
  18.5 2.5 stack.19
  20.9 13.0 %all-to-all-start = ((bf16[32,2,128,256]{3,2,1,0:T(8,128)(2,1)}), bf16[32,2,128,256]{3,2,1,0:T(8,128)(2,1)}, u32[]{:S(2)}, u32[]{:S(2)}) async-start(bf16[32,2,128,256]{3,2,1,0:T(8,128)(2,1)} %stack.19), calls=%async_computation | async-start | bytes 8388608 | tf_op jit(solution)/shard_map/all_to_all | solution.py:24
  33.9 0.0 reduce-scatter.3.cloned.1.call-start
  34.0 0.1 reshape.46
  34.1 94.7 %all-to-all-done = bf16[32,2,128,256]{3,2,1,0:T(8,128)(2,1)} async-done(((bf16[32,2,128,256]{3,2,1,0:T(8,128)(2,1)}), bf16[32,2,128,256]{3,2,1,0:T(8,128)(2,1)}, u32[]{:S(2)}, u32[]{:S(2)}) %all-to-all-start) | async-done | bytes 4194336 | tf_op jit(solution)/shard_map/all_to_all | solution.py:24
  128.8 8.2 %gather_fusion = bf16[96,128,256]{2,1,0:T(8,128)(2,1)} fusion(bf16[64,128,256]{2,1,0:T(8,128)(2,1)} %bitcast.3, s32[1024]{0:T(1024)S(1)} %pad_clamp_fusion), kind=kCustom, calls=%fused_computation.clone | custom fusion | bytes 12583296 | tf_op jit(solution)/shard_map/jit(_take)/gather | solution.py:38
  137.0 5.2 fusion.2
  142.2 0.0 reduce-scatter.3.cloned.1.call-update
  142.2 0.0 reduce-scatter.5.cloned.1.call-start
  142.3 37.0 %reduce-scatter.3.cloned.1.call-done = f32[128,256]{1,0:T(8,128)} async-done(((f32[1024,256]{1,0:T(8,128)}), f32[128,256]{1,0:T(8,128)}) %reduce-scatter.3.cloned.1.call-update) | async-done | bytes 131088 | tf_op jit(solution)/shard_map/reduce_scatter | solution.py:55
  179.3 1.6 convert_reduce_fusion
  180.9 5.5 collective-permute-start.1
  186.4 3.8 collective-permute-done.1
  190.3 0.5 stack.23
  190.8 95.0 %all_to_all.10 = bf16[32,2,128,256]{3,2,1,0:T(8,128)(2,1)} all-to-all(bf16[32,2,128,256]{3,2,1,0:T(8,128)(2,1)S(1)} %stack.23), channel_id=1, replica_groups=mesh['y_lo'=4,'core'=2,'y_hi'=2,'x'=4,'z'=8] {'x','z'}, dimensions={0} | all-to-all | bytes 8388608 | tf_op jit(solution)/shard_map/all_to_all | solution.py:24
  285.7 8.2 %gather_fusion.1 = bf16[96,128,256]{2,1,0:T(8,128)(2,1)} fusion(bf16[64,128,256]{2,1,0:T(8,128)(2,1)} %bitcast.34, s32[1024]{0:T(1024)S(1)} %pad_clamp_fusion), kind=kCustom, calls=%fused_computation.1.clone | custom fusion | bytes 12583296 | tf_op jit(solution)/shard_map/jit(_take)/gather | solution.py:38
  293.9 5.2 fusion
  299.1 0.0 reduce-scatter.5.cloned.1.call-update
  299.2 0.0 all-reduce.3.cloned.1.call-start
  299.2 44.0 %reduce-scatter.5.cloned.1.call-done = f32[128,256]{1,0:T(8,128)} async-done(((f32[1024,256]{1,0:T(8,128)}), f32[128,256]{1,0:T(8,128)}) %reduce-scatter.5.cloned.1.call-update) | async-done | bytes 131088 | tf_op jit(solution)/shard_map/reduce_scatter | solution.py:62
  343.2 1.1 convolution_bitcast_fusion
  344.3 0.7 pad_maximum_fusion
  345.0 0.0 all-reduce.3.cloned.1.call-update
  345.0 0.0 all-reduce.5.cloned.1.call-start
  345.1 153.4 %all-reduce.3.cloned.1.call-done = f32[257,256]{1,0:T(8,128)} async-done(((f32[257,256]{1,0:T(8,128)}), f32[257,256]{1,0:T(8,128)}) %all-reduce.3.cloned.1.call-update) | async-done | bytes 263184 | tf_op jit(solution)/shard_map/psum | solution.py:71
  498.5 1.7 convolution_convert_fusion
  500.2 111.6 %all-reduce.5.cloned.1.call-done = f32[257,256]{1,0:T(8,128)} async-done(((f32[257,256]{1,0:T(8,128)}), f32[257,256]{1,0:T(8,128)}) %all-reduce.5.cloned.1.call-update) | async-done | bytes 263184 | tf_op jit(solution)/shard_map/psum | solution.py:72
  611.9 1.3 slice.13
  613.1 1.7 slice.12
  (17 shorter events, 0.1 us)
Async XLA Ops:
  7.2 129.8 %copy-start = (bf16[1,8,1,12,128,128]{5,4,3,2,1,0:T(8,128)(2,1)S(1)}, bf16[1,8,1,12,128,128]{5,4,3,2,1,0:T(8,128)(2,1)}, u32[]{:S(2)}) copy-start(bf16[1,8,1,12,128,128]{5,4,3,2,1,0:T(8,128)(2,1)} %param.13) | copy-start | bytes 9437188
  8.4 10.0 %collective-permute-start = (bf16[128,256]{1,0:T(8,128)(2,1)S(1)}, bf16[128,256]{1,0:T(8,128)(2,1)S(1)}, u32[]{:S(2)}, u32[]{:S(2)}) collective-permute-start(bf16[128,256]{1,0:T(8,128)(2,1)S(1)} %convolution_convert_fusion.1), channel_id=1, source_target_pairs={{0,32},{32,0},{1,33},{33,1},{2,34},{34,2},{3,35},{35,3},{4,36},{36... | collective-permute-start | bytes 196616 | tf_op jit(solution)/shard_map/ppermute | solution.py:21
  18.5 15.5 %copy-start.4 = (s32[1,8,1,12]{3,2,1,0:T(1,128)S(1)}, s32[1,8,1,12]{3,2,1,0:T(1,128)}, u32[]{:S(2)}) copy-start(s32[1,8,1,12]{3,2,1,0:T(1,128)} %param.12) | copy-start | bytes 1156
  20.9 107.9 %all-to-all-start = ((bf16[32,2,128,256]{3,2,1,0:T(8,128)(2,1)}), bf16[32,2,128,256]{3,2,1,0:T(8,128)(2,1)}, u32[]{:S(2)}, u32[]{:S(2)}) async-start(bf16[32,2,128,256]{3,2,1,0:T(8,128)(2,1)} %stack.19), calls=%async_computation | async-start | bytes 8388608 | tf_op jit(solution)/shard_map/all_to_all | solution.py:24
  33.9 145.3 %reduce-scatter.3.cloned.1.call-start = ((), (), s32[]{:S(2)}) async-start(), calls=%async_computation.4 | async-start | bytes 1179648 | tf_op jit(solution)/shard_map/reduce_scatter | solution.py:55
  137.0 42.3 %copy-start.3 = (bf16[128,256]{1,0:T(8,128)(2,1)S(1)}, bf16[128,256]{1,0:T(8,128)(2,1)}, u32[]{:S(2)}) copy-start(bf16[128,256]{1,0:T(8,128)(2,1)} %param.11) | copy-start | bytes 196612
  137.0 42.3 %copy-start.5 = (f32[256]{0:T(256)S(1)}, f32[256]{0:T(256)}, u32[]{:S(2)}) copy-start(f32[256]{0:T(256)} %param.10) | copy-start | bytes 3076
  142.2 200.9 %reduce-scatter.5.cloned.1.call-start = ((), (), s32[]{:S(2)}) async-start(), calls=%async_computation.5 | async-start | bytes 1179648 | tf_op jit(solution)/shard_map/reduce_scatter | solution.py:62
  180.9 9.3 %collective-permute-start.1 = (bf16[128,256]{1,0:T(8,128)(2,1)S(1)}, bf16[128,256]{1,0:T(8,128)(2,1)S(1)}, u32[]{:S(2)}, u32[]{:S(2)}) collective-permute-start(bf16[128,256]{1,0:T(8,128)(2,1)S(1)} %get-tuple-element.6), channel_id=1, source_target_pairs={{0,32},{32,0},{1,33},{33,1},{2,34},{34,2},{3,35},{35,3},{4,36},{36... | collective-permute-start | bytes 196616 | tf_op jit(solution)/shard_map/ppermute | solution.py:21
  293.9 49.2 %copy-start.2 = (bf16[128,256]{1,0:T(8,128)(2,1)S(1)}, bf16[128,256]{1,0:T(8,128)(2,1)}, u32[]{:S(2)}) copy-start(bf16[128,256]{1,0:T(8,128)(2,1)} %param.8) | copy-start | bytes 196612
  293.9 204.5 %copy-start.1 = (bf16[256,256]{1,0:T(8,128)(2,1)S(1)}, bf16[256,256]{1,0:T(8,128)(2,1)}, u32[]{:S(2)}) copy-start(bf16[256,256]{1,0:T(8,128)(2,1)} %param.9) | copy-start | bytes 393220
  299.2 199.3 %all-reduce.3.cloned.1.call-start = ((), (), s32[]{:S(2)}) async-start(), calls=%async_computation.6 | async-start | bytes 540672 | tf_op jit(solution)/shard_map/psum | solution.py:71
  345.0 266.8 %all-reduce.5.cloned.1.call-start = ((), (), s32[]{:S(2)}) async-start(), calls=%async_computation.7 | async-start | bytes 540672 | tf_op jit(solution)/shard_map/psum | solution.py:72
Sparse Core Ops, SparseCore 0:
  142.3 36.8 reduce-scatter.2
  299.3 43.8 reduce-scatter.4
  346.6 151.7 all-reduce.2
  500.6 111.1 all-reduce.4
